TPU v7x, 32 devices: a whole 2x2x4 slice. The times are simulated.
32 devices in a mesh: dp: 2 (over y), seq: 16 (over z, x, core).
Axes of the slice: x: 2, y: 2, z: 4, core: 2. Of those that a mesh axis runs over, the one named last changes fastest.
Arguments:
- tokens: bfloat16 [2, 4096, 768], P('dp', 'seq'), may hold values from -6 to 6
- segment_ids: int32 [2, 4096], P('dp', 'seq'), may hold values from 0 to 7, never falling along the last dimension, each value on 1 to 2048 neighbouring positions
- features: bfloat16 [12, 64, 256], replicated, may hold values from -6 to 6
- query_weight: bfloat16 [768, 768], replicated, may hold values from -0.15625 to 0.15625
- key_weight: bfloat16 [768, 768], replicated, may hold values from -0.15625 to 0.15625
- value_weight: bfloat16 [768, 768], replicated, may hold values from -0.21875 to 0.21875
- out_weight: bfloat16 [768, 768], replicated, may hold values from -0.875 to 0.875
- up_weight: bfloat16 [768, 3072], replicated, may hold values from -0.21875 to 0.21875
- down_weight: bfloat16 [3072, 768], replicated, may hold values from -0.109375 to 0.109375
- first_gain: float32 [768], replicated, may hold values from 0.1 to 1.9
- first_bias: float32 [768], replicated, may hold values from -3 to 3
- second_gain: float32 [768], replicated, may hold values from 0.1 to 1.9
- second_bias: float32 [768], replicated, may hold values from -3 to 3
- cotangent: bfloat16 [2, 4096, 768], P('dp', 'seq'), may hold values from -6 to 6
Outputs:
- output: bfloat16 [2, 4096, 768], P('dp', 'seq')
- grad_tokens: bfloat16 [2, 4096, 768], P('dp', 'seq')
- grad_query: float32 [768, 768], replicated
- grad_key: float32 [768, 768], replicated
- grad_value: float32 [768, 768], replicated
- grad_out: float32 [768, 768], replicated
- grad_up: float32 [768, 3072], replicated
- grad_down: float32 [3072, 768], replicated
- grad_first_gain: float32 [768], replicated
- grad_first_bias: float32 [768], replicated
- grad_second_gain: float32 [768], replicated
- grad_second_bias: float32 [768], replicated
Inputs may be any that keep to these rules, and one draw needn't show every extreme that they name: `segment_ids`: in each row the ids never fall, every id from 0 to 7 occurs, each on 1 to 2048 positions, and one on exactly 2048.
All inputs are finite; a program needn't handle non-finite values.
Results may differ from a plain program's by a relative error of at most 0.02.
Values sent between devices are 32-bit elements; how exact they have to be, the bound alone decides.
No kernel may reach another device: no remote copies, remote signals or barrier semaphores. Data moves between devices by JAX's collectives and lax.ppermute only.
A program may use at most 320 MiB of HBM per device.

v0:
```python
from functools import partial
import jax
import jax.numpy as jnp
from jax import lax
from jax.sharding import PartitionSpec as P

SEGS = 8
EPSILON = 1e-06
HIGHEST = lax.Precision.HIGHEST


def carried_in(value, axis, combine, identity, reverse):
    length, place = (lax.axis_size(axis), lax.axis_index(axis))
    everything = jax.tree.map(lambda part: lax.all_gather(part, axis), value)
    start = jax.tree.map(
        lambda part, zero: jnp.broadcast_to(jnp.asarray(zero, part.dtype), part.shape),
        value,
        identity,
    )

    def hop(k, before):
        at = length - 1 - k if reverse else k
        reached = at > place if reverse else at < place
        new = combine(before, jax.tree.map(lambda part: part[at], everything))
        return jax.tree.map(lambda a, b: jnp.where(reached, a, b), new, before)

    return lax.fori_loop(0, length, hop, start)


def norm_forward(hidden, norm_gain, norm_bias):
    row_mean = jnp.mean(hidden, -1, keepdims=True)
    centered = hidden - row_mean
    variance = jnp.mean(centered * centered, -1, keepdims=True)
    inv_std = lax.rsqrt(variance + EPSILON)
    normed = centered * inv_std
    return (normed * norm_gain + norm_bias, normed, inv_std)


def norm_backward(upstream, normed, inv_std, norm_gain):
    scaled = upstream * norm_gain
    grad_hidden = inv_std * (
        scaled
        - jnp.mean(scaled, -1, keepdims=True)
        - normed * jnp.mean(scaled * normed, -1, keepdims=True)
    )
    return (grad_hidden, jnp.sum(upstream * normed, 0), jnp.sum(upstream, 0))


def feature_map(projected, features):
    head_dim = projected.shape[-1]
    feat_count = features.shape[-1]
    inner_u = jnp.einsum("rthe,hem->rthm", projected, features, preferred_element_type=jnp.float32)
    widened = projected.astype(jnp.float32)
    square = jnp.sum(widened * widened, -1, keepdims=True)
    return jnp.exp(
        inner_u * head_dim ** (-0.25) - 0.5 * head_dim ** (-0.5) * square
    ) * feat_count ** (-0.5)


def feature_back(grad_feat, feat_vals, projected, features):
    head_dim = projected.shape[-1]
    weighted = grad_feat * feat_vals
    grad_inner = (weighted * head_dim ** (-0.25)).astype(jnp.bfloat16)
    grad_proj = jnp.einsum(
        "rthm,hem->rthe", grad_inner, features, preferred_element_type=jnp.float32
    )
    grad_proj = grad_proj - head_dim ** (-0.5) * projected.astype(jnp.float32) * jnp.sum(
        weighted, -1, keepdims=True
    )
    return grad_proj.astype(jnp.bfloat16)


def join_forward(earlier, later):
    earlier_kv, earlier_z, earlier_first, earlier_last, earlier_whole = earlier
    later_kv, later_z, later_first, later_last, later_whole = later
    matched = (earlier_last == later_first) | (earlier_last < 0) | (later_first < 0)
    joined = (later_whole == 1) & matched
    kv_part = jnp.where(joined[:, None, None, None], earlier_kv + later_kv, later_kv)
    z_part = jnp.where(joined[:, None, None], earlier_z + later_z, later_z)
    first_id = jnp.where(earlier_first < 0, later_first, earlier_first)
    last_id = jnp.where(later_last < 0, earlier_last, later_last)
    whole_run = earlier_whole * later_whole * matched.astype(jnp.int32)
    return (kv_part, z_part, first_id, last_id, whole_run)


def join_backward(earlier, later):
    earlier_kv, earlier_z, earlier_first, earlier_last, earlier_whole = earlier
    later_kv, later_z, later_first, later_last, later_whole = later
    matched = (later_last == earlier_first) | (later_last < 0) | (earlier_first < 0)
    joined = (later_whole == 1) & matched
    kv_part = jnp.where(joined[:, None, None, None], earlier_kv + later_kv, later_kv)
    z_part = jnp.where(joined[:, None, None], earlier_z + later_z, later_z)
    first_id = jnp.where(later_first < 0, earlier_first, later_first)
    last_id = jnp.where(earlier_last < 0, later_last, earlier_last)
    whole_run = earlier_whole * later_whole * matched.astype(jnp.int32)
    return (kv_part, z_part, first_id, last_id, whole_run)


def segment_totals(local_kv, local_z, segment_ids):
    row_count = local_kv.shape[0]
    labels = jnp.arange(local_kv.shape[1], dtype=jnp.int32)
    first_id = segment_ids[:, 0]
    last_id = segment_ids[:, -1]
    whole_run = (first_id == last_id).astype(jnp.int32)
    is_last = last_id[:, None] == labels[None, :]
    is_first = first_id[:, None] == labels[None, :]
    tail_kv = jnp.sum(jnp.where(is_last[:, :, None, None, None], local_kv, 0.0), 1)
    tail_z = jnp.sum(jnp.where(is_last[:, :, None, None], local_z, 0.0), 1)
    lead_kv = jnp.sum(jnp.where(is_first[:, :, None, None, None], local_kv, 0.0), 1)
    lead_z = jnp.sum(jnp.where(is_first[:, :, None, None], local_z, 0.0), 1)
    identity = (
        jnp.zeros_like(tail_kv),
        jnp.zeros_like(tail_z),
        -jnp.ones((row_count,), jnp.int32),
        -jnp.ones((row_count,), jnp.int32),
        jnp.ones((row_count,), jnp.int32),
    )
    before = carried_in(
        (tail_kv, tail_z, first_id, last_id, whole_run), "seq", join_forward, identity, False
    )
    behind = carried_in(
        (lead_kv, lead_z, first_id, last_id, whole_run), "seq", join_backward, identity, True
    )
    from_before = before[3][:, None] == labels[None, :]
    from_behind = behind[2][:, None] == labels[None, :]
    total_kv = (
        local_kv
        + jnp.where(from_before[:, :, None, None, None], before[0][:, None], 0.0)
        + jnp.where(from_behind[:, :, None, None, None], behind[0][:, None], 0.0)
    )
    total_z = (
        local_z
        + jnp.where(from_before[:, :, None, None], before[1][:, None], 0.0)
        + jnp.where(from_behind[:, :, None, None], behind[1][:, None], 0.0)
    )
    return (total_kv, total_z)


def body(
    tokens,
    segment_ids,
    features,
    query_weight,
    key_weight,
    value_weight,
    out_weight,
    up_weight,
    down_weight,
    first_gain,
    first_bias,
    second_gain,
    second_bias,
    cotangent,
):
    row_count, row_len, width_d = tokens.shape
    head_count, head_dim = (features.shape[0], features.shape[1])
    token_count = row_count * row_len
    tokens_flat = tokens.reshape(token_count, width_d)

    def project(weight):
        product = jnp.dot(tokens_flat, weight, preferred_element_type=jnp.float32)
        return product.astype(jnp.bfloat16).reshape(row_count, row_len, head_count, head_dim)

    queries = project(query_weight)
    keys_b = project(key_weight)
    values_b = project(value_weight)
    feat_q = feature_map(queries, features)
    feat_k = feature_map(keys_b, features)
    feat_q_b = feat_q.astype(jnp.bfloat16)
    feat_k_b = feat_k.astype(jnp.bfloat16)
    labels = jnp.arange(SEGS, dtype=jnp.int32)
    onehot = segment_ids[:, :, None] == labels[None, None, :]
    mask_b = onehot.astype(jnp.bfloat16)
    mask_f = onehot.astype(jnp.float32)
    masked_values = mask_b[:, :, :, None, None] * values_b[:, :, None]
    local_kv = jnp.einsum(
        "rthm,rtshe->rshme", feat_k_b, masked_values, preferred_element_type=jnp.float32
    )
    local_z = jnp.einsum("rts,rthm->rshm", mask_b, feat_k_b, preferred_element_type=jnp.float32)
    kv_total, z_total = segment_totals(local_kv, local_z, segment_ids)
    kv_b = kv_total.astype(jnp.bfloat16)
    per_segment = jnp.einsum(
        "rthm,rshme->rtshe", feat_q_b, kv_b, preferred_element_type=jnp.float32
    )
    numer = jnp.sum(jnp.where(onehot[:, :, :, None, None], per_segment, 0.0), 2)
    z_picked = jnp.einsum("rts,rshm->rthm", mask_f, z_total, precision=HIGHEST)
    denom = jnp.sum(feat_q_b.astype(jnp.float32) * z_picked, -1)
    attention = numer / denom[..., None]
    attention_b = attention.astype(jnp.bfloat16).reshape(token_count, width_d)
    hidden_one = tokens_flat.astype(jnp.float32) + jnp.dot(
        attention_b, out_weight, preferred_element_type=jnp.float32
    )
    normed_one, unit_one, inv_one = norm_forward(hidden_one, first_gain, first_bias)
    normed_one_b = normed_one.astype(jnp.bfloat16)
    inner_f = jnp.dot(normed_one_b, up_weight, preferred_element_type=jnp.float32)
    activated, gelu_pull = jax.vjp(partial(jax.nn.gelu, approximate=False), inner_f)
    activated_b = activated.astype(jnp.bfloat16)
    hidden_two = normed_one + jnp.dot(activated_b, down_weight, preferred_element_type=jnp.float32)
    result, unit_two, inv_two = norm_forward(hidden_two, second_gain, second_bias)
    upstream = cotangent.reshape(token_count, width_d).astype(jnp.float32)
    grad_two, grad_gain_two, grad_bias_two = norm_backward(upstream, unit_two, inv_two, second_gain)
    grad_branch = grad_two.astype(jnp.bfloat16)
    grad_down_w = jnp.einsum(
        "nf,nd->fd", activated_b, grad_branch, preferred_element_type=jnp.float32
    )
    grad_act = jnp.einsum("nd,fd->nf", grad_branch, down_weight, preferred_element_type=jnp.float32)
    (grad_inner,) = gelu_pull(grad_act)
    grad_inner_b = grad_inner.astype(jnp.bfloat16)
    grad_up_w = jnp.einsum(
        "nd,nf->df", normed_one_b, grad_inner_b, preferred_element_type=jnp.float32
    )
    grad_normed = grad_two + jnp.einsum(
        "nf,df->nd", grad_inner_b, up_weight, preferred_element_type=jnp.float32
    )
    grad_one, grad_gain_one, grad_bias_one = norm_backward(
        grad_normed, unit_one, inv_one, first_gain
    )
    grad_attn_out = grad_one.astype(jnp.bfloat16)
    grad_out_w = jnp.einsum(
        "nd,ne->de", attention_b, grad_attn_out, preferred_element_type=jnp.float32
    )
    grad_attention = jnp.einsum(
        "ne,de->nd", grad_attn_out, out_weight, preferred_element_type=jnp.float32
    )
    grad_attention = grad_attention.reshape(row_count, row_len, head_count, head_dim)
    grad_numer_b = (grad_attention / denom[..., None]).astype(jnp.bfloat16)
    grad_denom = -jnp.sum(grad_attention * attention, -1) / denom
    masked_grad = mask_b[:, :, :, None, None] * grad_numer_b[:, :, None]
    grad_feat_q = jnp.einsum(
        "rtshe,rshme->rthm", masked_grad, kv_b, preferred_element_type=jnp.float32
    )
    grad_feat_q = grad_feat_q + z_picked * grad_denom[..., None]
    local_grad_kv = jnp.einsum(
        "rthm,rtshe->rshme", feat_q_b, masked_grad, preferred_element_type=jnp.float32
    )
    local_grad_z = jnp.einsum(
        "rts,rthm->rshm",
        mask_f,
        feat_q_b.astype(jnp.float32) * grad_denom[..., None],
        precision=HIGHEST,
    )
    grad_kv_total, grad_z_total = segment_totals(local_grad_kv, local_grad_z, segment_ids)
    grad_kv_b = grad_kv_total.astype(jnp.bfloat16)
    grad_feat_k = jnp.einsum(
        "rtshe,rshme->rthm", masked_values, grad_kv_b, preferred_element_type=jnp.float32
    )
    grad_feat_k = grad_feat_k + jnp.einsum(
        "rts,rshm->rthm", mask_f, grad_z_total, precision=HIGHEST
    )
    value_terms = jnp.einsum(
        "rthm,rshme->rtshe", feat_k_b, grad_kv_b, preferred_element_type=jnp.float32
    )
    grad_values = jnp.sum(jnp.where(onehot[:, :, :, None, None], value_terms, 0.0), 2).astype(
        jnp.bfloat16
    )
    grad_queries = feature_back(grad_feat_q, feat_q, queries, features)
    grad_keys = feature_back(grad_feat_k, feat_k, keys_b, features)
    grad_q_flat = grad_queries.reshape(token_count, width_d)
    grad_k_flat = grad_keys.reshape(token_count, width_d)
    grad_v_flat = grad_values.reshape(token_count, width_d)
    grad_query_w = jnp.einsum(
        "nd,ne->de", tokens_flat, grad_q_flat, preferred_element_type=jnp.float32
    )
    grad_key_w = jnp.einsum(
        "nd,ne->de", tokens_flat, grad_k_flat, preferred_element_type=jnp.float32
    )
    grad_value_w = jnp.einsum(
        "nd,ne->de", tokens_flat, grad_v_flat, preferred_element_type=jnp.float32
    )
    grad_input = (
        grad_one
        + jnp.einsum("ne,de->nd", grad_q_flat, query_weight, preferred_element_type=jnp.float32)
        + jnp.einsum("ne,de->nd", grad_k_flat, key_weight, preferred_element_type=jnp.float32)
        + jnp.einsum("ne,de->nd", grad_v_flat, value_weight, preferred_element_type=jnp.float32)
    )
    local_grads = (
        grad_query_w,
        grad_key_w,
        grad_value_w,
        grad_out_w,
        grad_up_w,
        grad_down_w,
        grad_gain_one,
        grad_bias_one,
        grad_gain_two,
        grad_bias_two,
    )
    shares = (
        lax.psum_scatter(local_grads[0], "seq", scatter_dimension=0, tiled=True),
        lax.psum_scatter(local_grads[1], "seq", scatter_dimension=0, tiled=True),
        lax.psum_scatter(local_grads[2], "seq", scatter_dimension=0, tiled=True),
        lax.psum_scatter(local_grads[3], "seq", scatter_dimension=0, tiled=True),
        lax.psum_scatter(local_grads[4], "seq", scatter_dimension=0, tiled=True),
        lax.psum_scatter(local_grads[5], "seq", scatter_dimension=0, tiled=True),
        lax.psum_scatter(local_grads[6], "seq", scatter_dimension=0, tiled=True),
        lax.psum_scatter(local_grads[7], "seq", scatter_dimension=0, tiled=True),
        lax.psum_scatter(local_grads[8], "seq", scatter_dimension=0, tiled=True),
        lax.psum_scatter(local_grads[9], "seq", scatter_dimension=0, tiled=True),
    )
    shares = lax.psum(
        (
            shares[0],
            shares[1],
            shares[2],
            shares[3],
            shares[4],
            shares[5],
            shares[6],
            shares[7],
            shares[8],
            shares[9],
        ),
        "dp",
    )
    summed = (
        lax.all_gather(shares[0], "seq", axis=0, tiled=True),
        lax.all_gather(shares[1], "seq", axis=0, tiled=True),
        lax.all_gather(shares[2], "seq", axis=0, tiled=True),
        lax.all_gather(shares[3], "seq", axis=0, tiled=True),
        lax.all_gather(shares[4], "seq", axis=0, tiled=True),
        lax.all_gather(shares[5], "seq", axis=0, tiled=True),
        lax.all_gather(shares[6], "seq", axis=0, tiled=True),
        lax.all_gather(shares[7], "seq", axis=0, tiled=True),
        lax.all_gather(shares[8], "seq", axis=0, tiled=True),
        lax.all_gather(shares[9], "seq", axis=0, tiled=True),
    )
    return (
        result.astype(jnp.bfloat16).reshape(row_count, row_len, width_d),
        grad_input.astype(jnp.bfloat16).reshape(row_count, row_len, width_d),
        summed[0],
        summed[1],
        summed[2],
        summed[3],
        summed[4],
        summed[5],
        summed[6],
        summed[7],
        summed[8],
        summed[9],
    )


def solution(mesh):
    placed = (
        P("dp", "seq", None),
        P("dp", "seq"),
        P(),
        P(),
        P(),
        P(),
        P(),
        P(),
        P(),
        P(),
        P(),
        P(),
        P(),
        P("dp", "seq", None),
    )
    return jax.shard_map(
        body,
        mesh=mesh,
        in_specs=placed,
        out_specs=(
            P("dp", "seq", None),
            P("dp", "seq", None),
            P(),
            P(),
            P(),
            P(),
            P(),
            P(),
            P(),
            P(),
            P(),
            P(),
        ),
        check_vma=False,
    )
```

profile of v0, /device:TPU:0, one launch (start us, length us, event | category | flops | bytes accessed | tf_op | source)
XLA Modules:
  0.0 1851.2 jit_solution(2164421294902823707)
XLA Ops:
  17.5 5.5 fusion.14
  29.0 14.8 all-reduce.11
  51.6 21.3 %all-gather.9 = f32[16,12,256]{2,1,0:T(8,128)} all-gather(f32[1,12,256]{2,1,0:T(8,128)S(1)} %bitcast.471), channel_id=5, replica_groups=mesh['dp'=2,'seq'=16] {'seq'}, dimensions={0}, use_global_device_ids=true | all-gather | bytes 208896 | tf_op jit(solution)/shard_map/all_gather | solution.py:14
  72.9 22.4 %all-gather.8 = f32[16,12,256]{2,1,0:T(8,128)} all-gather(f32[1,12,256]{2,1,0:T(8,128)S(1)} %bitcast.470), channel_id=3, replica_groups=mesh['dp'=2,'seq'=16] {'seq'}, dimensions={0}, use_global_device_ids=true | all-gather | bytes 208896 | tf_op jit(solution)/shard_map/all_gather | solution.py:14
  98.3 31.5 %all-gather.37.cloned.1.call-done = f32[192,256,64]{1,2,0:T(8,128)} async-done(((f32[12,256,64]{1,2,0:T(8,128)}), f32[192,256,64]{1,2,0:T(8,128)}) %all-gather.37.cloned.1.call-update) | async-done | bytes 12582928 | tf_op jit(solution)/shard_map/all_gather | solution.py:14
  129.8 174.6 %while.77 = (s32[]{:T(128)}, f32[1,12,256,64]{3,2,1,0:T(8,128)}, f32[1,12,256]{2,1,0:T(8,128)}, s32[1]{0:T(128)}, s32[]{:T(128)}, /*index=5*/s32[16,1]{0,1:T(1,1...) while((s32[]{:T(128)}, f32[1,12,256,64]{3,2,1,0:T(8,128)}, ...), condition=%wide.region_8.9_spmd.clone, body=%wide.region_7.8_spmd.clone.sunk | while | flops 798738 | bytes 5640575 | solution.py:27
  307.1 173.8 %while.76 = (s32[]{:T(128)}, f32[1,12,256,64]{3,2,1,0:T(8,128)}, f32[1,12,256]{2,1,0:T(8,128)S(1)}, s32[1]{0:T(128)}, s32[]{:T(128)}, /*index=5*/s32[16,1]{0,1:T...) while((s32[]{:T(128)}, f32[1,12,256,64]{3,2,1,0:T(8,128)}, ...), condition=%wide.region_4.5_spmd.clone, body=%wide.region_3.4_spmd.clone.sunk | while | flops 798734 | bytes 5542153 | solution.py:27
  482.9 4.4 fusion.31
  494.2 8.1 multiply_convert_fusion.2
  514.0 5.5 fusion.10
  520.4 5.8 fusion.172
  535.2 22.8 %all-gather.11 = f32[16,12,256]{2,1,0:T(8,128)} all-gather(f32[1,12,256]{2,1,0:T(8,128)S(1)} %bitcast.469), channel_id=9, replica_groups=mesh['dp'=2,'seq'=16] {'seq'}, dimensions={0}, use_global_device_ids=true | all-gather | bytes 208896 | tf_op jit(solution)/shard_map/all_gather | solution.py:14
  558.1 20.8 %all-gather.10 = f32[16,12,256]{2,1,0:T(8,128)} all-gather(f32[1,12,256]{2,1,0:T(8,128)S(1)} %bitcast.468), channel_id=7, replica_groups=mesh['dp'=2,'seq'=16] {'seq'}, dimensions={0}, use_global_device_ids=true | all-gather | bytes 208896 | tf_op jit(solution)/shard_map/all_gather | solution.py:14
  578.9 41.9 %all-gather.41.cloned.1.call-done = f32[192,256,64]{1,2,0:T(8,128)} async-done(((f32[12,256,64]{1,2,0:T(8,128)}), f32[192,256,64]{1,2,0:T(8,128)}) %all-gather.41.cloned.1.call-update) | async-done | bytes 12582928 | tf_op jit(solution)/shard_map/all_gather | solution.py:14
  620.8 172.1 %while.79 = (s32[]{:T(128)}, f32[1,12,256,64]{3,2,1,0:T(8,128)}, f32[1,12,256]{2,1,0:T(8,128)}, s32[1]{0:T(128)}, s32[]{:T(128)}, /*index=5*/s32[16,1]{0,1:T(1,1...) while((s32[]{:T(128)}, f32[1,12,256,64]{3,2,1,0:T(8,128)}, ...), condition=%wide.region_29.30_spmd.clone, body=%wide.region_28.29_spmd.clone.sunk | while | flops 798738 | bytes 5640575 | solution.py:27
  793.0 171.2 %while.78 = (s32[]{:T(128)}, f32[1,12,256,64]{3,2,1,0:T(8,128)}, f32[1,12,256]{2,1,0:T(8,128)S(1)}, s32[1]{0:T(128)}, s32[]{:T(128)}, /*index=5*/s32[16,1]{0,1:T...) while((s32[]{:T(128)}, f32[1,12,256,64]{3,2,1,0:T(8,128)}, ...), condition=%wide.region_25.26_spmd.clone, body=%wide.region_24.25_spmd.clone.sunk | while | flops 798734 | bytes 5542153 | solution.py:27
  970.1 4.2 fusion.32
  993.4 6.8 fusion.156
  1002.0 6.0 fusion.116
  1010.0 34.8 %reduce-scatter.21.cloned.1.call-done = f32[48,768]{1,0:T(8,128)} async-done(((f32[768,768]{1,0:T(8,128)}), f32[48,768]{1,0:T(8,128)}) %reduce-scatter.21.cloned.1.call-update) | async-done | bytes 147472
  1046.7 64.7 %reduce-scatter.23.cloned.1.call-done = f32[48,768]{1,0:T(8,128)} async-done(((f32[768,768]{1,0:T(8,128)}), f32[48,768]{1,0:T(8,128)}) %reduce-scatter.23.cloned.1.call-update) | async-done | bytes 147472
  1113.2 64.7 %reduce-scatter.13.cloned.1.call-done = f32[48,768]{1,0:T(8,128)} async-done(((f32[768,768]{1,0:T(8,128)}), f32[48,768]{1,0:T(8,128)}) %reduce-scatter.13.cloned.1.call-update) | async-done | bytes 147472 | tf_op jit(solution)/shard_map/reduce_scatter | solution.py:292
  1177.9 115.0 %reduce-scatter.15.cloned.1.call-done = f32[48,3072]{1,0:T(8,128)} async-done(((f32[768,3072]{1,0:T(8,128)}), f32[48,3072]{1,0:T(8,128)}) %reduce-scatter.15.cloned.1.call-update) | async-done | bytes 589840 | tf_op jit(solution)/shard_map/reduce_scatter | solution.py:293
  1292.8 115.4 %reduce-scatter.17.cloned.1.call-done = f32[192,768]{1,0:T(8,128)} async-done(((f32[3072,768]{1,0:T(8,128)}), f32[192,768]{1,0:T(8,128)}) %reduce-scatter.17.cloned.1.call-update) | async-done | bytes 589840 | tf_op jit(solution)/shard_map/reduce_scatter | solution.py:294
  1408.3 74.8 %all-reduce.18.cloned.1.call-done = (f32[48,768]{0,1:T(8,128)}, f32[48,768]{0,1:T(8,128)}, f32[48,768]{0,1:T(8,128)}, f32[48,768]{1,0:T(8,128)}, f32[48,3072]{1,0:T(8,128)}, /*index=5*/f32[192,768]{1,0:T(8,128)}) async-done(((f32[48,768]{0,1:T(8,128)}, f32[48,768]{0,1:T(8,128)}, f32[48,768]{0,1:T(8,128)}, f32[48,768]{1,0:T(8,128)}, f32[48,3072]{1,0:T(8,128)}, /*index=5*/f32[192,768]{1,0:T(8,128)}), ...) | async-done | bytes 1769488 | tf_op jit(solution)/shard_map/psum | solution.py:300
  1492.9 61.7 %all-reduce.13 = (f32[768]{0:T(1024)}, f32[768]{0:T(1024)}, f32[768]{0:T(1024)}, f32[768]{0:T(1024)}) all-reduce(f32[768]{0:T(1024)S(1)} %copy-done.94, f32[768]{0:T(1024)S(1)} %copy-done.95, f32[768]{0:T(1024)S(1)} %copy-done.76, f32[768]{0:T(1024)S(1)} %convert_reduce_fusion), channel_id=16, replica_groups=mesh['dp'=2,'seq'=16] {'seq'}, use_global_device_ids=true, to_apply=%region_45.46.clone | all-reduce | flops 3072 | bytes 24576
  1557.6 5.4 all-reduce.14
  1566.4 58.2 %all-reduce.12 = (f32[768]{0:T(1024)}, f32[768]{0:T(1024)}, f32[768]{0:T(1024)}, f32[768]{0:T(1024)}) all-reduce(f32[768]{0:T(1024)S(1)} %dynamic-update-slice.3, f32[768]{0:T(1024)S(1)} %dynamic-update-slice.4, f32[768]{0:T(1024)S(1)} %dynamic-update-slice.5, f32[768]{0:T(1024)S(1)} %dynamic-update-slice.6), channel_id=1, replica_groups=mesh['dp'=2,'seq'=16] {'seq'}, use_global_device_ids=true, to_apply=%add.3 | all-reduce | flops 3072 | bytes 24576
  1627.4 32.4 %all-gather.29.cloned.1.call-done = f32[768,768]{1,0:T(8,128)} async-done(((f32[48,768]{1,0:T(8,128)}), f32[768,768]{1,0:T(8,128)}) %all-gather.29.cloned.1.call-update) | async-done | bytes 2359312 | tf_op jit(solution)/shard_map/all_gather | solution.py:319
  1659.7 81.8 %all-gather.31.cloned.1.call-done = f32[768,3072]{1,0:T(8,128)} async-done(((f32[48,3072]{1,0:T(8,128)}), f32[768,3072]{1,0:T(8,128)}) %all-gather.31.cloned.1.call-update) | async-done | bytes 9437200 | tf_op jit(solution)/shard_map/all_gather | solution.py:320
  1741.5 81.5 %all-gather.33.cloned.1.call-done = f32[3072,768]{1,0:T(8,128)} async-done(((f32[192,768]{1,0:T(8,128)}), f32[3072,768]{1,0:T(8,128)}) %all-gather.33.cloned.1.call-update) | async-done | bytes 9437200 | tf_op jit(solution)/shard_map/all_gather | solution.py:321
  1836.4 8.1 copy.216
  (858 shorter events, 608.4 us)
Async XLA Ops:
  7.2 485.1 %copy-start = (bf16[768,768]{1,0:T(8,128)(2,1)S(1)}, bf16[768,768]{1,0:T(8,128)(2,1)}, u32[]{:S(2)}) copy-start(bf16[768,768]{1,0:T(8,128)(2,1)} %param.28) | copy-start | bytes 3538948
  7.2 122.6 %all-gather.37.cloned.1.call-start = ((), (), s32[]{:S(2)}) async-start(), calls=%async_computation.16 | async-start | bytes 13369344 | tf_op jit(solution)/shard_map/all_gather | solution.py:14
  23.0 26.7 %copy-start.18 = (bf16[1,256,12,256]{1,3,2,0:T(8,128)(2,1)S(1)}, bf16[1,256,12,256]{1,3,2,0:T(8,128)(2,1)}, u32[]{:S(2)}) copy-start(bf16[1,256,12,256]{1,3,2,0:T(8,128)(2,1)} %copy-done.17) | copy-start | bytes 4718596
  23.0 284.1 %all-gather.35.cloned.1.call-start = ((), (), s32[]{:S(2)}) async-start(), calls=%async_computation.15 | async-start | bytes 13369344 | tf_op jit(solution)/shard_map/all_gather | solution.py:14
  23.8 597.0 %all-gather.41.cloned.1.call-start = ((), (), s32[]{:S(2)}) async-start(), calls=%async_computation.18 | async-start | bytes 13369344 | tf_op jit(solution)/shard_map/all_gather | solution.py:14
  47.5 50.8 %copy-start.15 = (f32[256,768]{0,1:T(8,128)}, f32[256,768]{0,1:T(8,128)S(1)}, u32[]{:S(2)}) copy-start(f32[256,768]{0,1:T(8,128)S(1)} %copy.83) | copy-start | bytes 2359300
  49.7 46.3 %copy-start.23 = (bf16[12,64,256]{2,1,0:T(8,128)(2,1)S(1)}, bf16[12,64,256]{2,1,0:T(8,128)(2,1)}, u32[]{:S(2)}) copy-start(bf16[12,64,256]{2,1,0:T(8,128)(2,1)} %param.24) | copy-start | bytes 1179652
  49.7 46.3 %copy-start.46 = (bf16[256,768]{0,1:T(8,128)(2,1)S(1)}, bf16[256,768]{0,1:T(8,128)(2,1)}, u32[]{:S(2)}) copy-start(bf16[256,768]{0,1:T(8,128)(2,1)} %copy.82) | copy-start | bytes 1179652
  491.1 22.8 %copy-start.52 = (f32[256,12]{0,1:T(8,128)}, f32[256,12]{0,1:T(8,128)S(1)}, u32[]{:S(2)}) copy-start(f32[256,12]{0,1:T(8,128)S(1)} %get-tuple-element.1168) | copy-start | bytes 36868
  491.1 22.9 %copy-start.20 = (bf16[1,256,12,256]{1,3,2,0:T(8,128)(2,1)}, bf16[1,256,12,256]{1,3,2,0:T(8,128)(2,1)S(1)}, u32[]{:S(2)}) copy-start(bf16[1,256,12,256]{1,3,2,0:T(8,128)(2,1)S(1)} %get-tuple-element.1169) | copy-start | bytes 4718596
  493.1 19.0 %copy-start.8 = (f32[256,768]{1,0:T(8,128)}, f32[256,768]{1,0:T(8,128)S(1)}, u32[]{:S(2)}) copy-start(f32[256,768]{1,0:T(8,128)S(1)} %get-tuple-element.1191) | copy-start | bytes 2359300
  519.5 273.4 %all-gather.39.cloned.1.call-start = ((), (), s32[]{:S(2)}) async-start(), calls=%async_computation.17 | async-start | bytes 13369344 | tf_op jit(solution)/shard_map/all_gather | solution.py:14
  520.1 488.1 %reduce-scatter.19.cloned.1.call-start = ((), (), s32[]{:S(2)}) async-start(), calls=%async_computation.19 | async-start | bytes 2506752
  578.9 466.0 %reduce-scatter.21.cloned.1.call-start = ((), (), s32[]{:S(2)}) async-start(), calls=%async_computation.20 | async-start | bytes 2506752
  982.3 129.0 %reduce-scatter.23.cloned.1.call-start = ((), (), s32[]{:S(2)}) async-start(), calls=%async_computation.21 | async-start | bytes 2506752
  991.2 186.7 %reduce-scatter.13.cloned.1.call-start = ((), (), s32[]{:S(2)}) async-start(), calls=%async_computation.9 | async-start | bytes 2506752 | tf_op jit(solution)/shard_map/reduce_scatter | solution.py:292
  993.3 299.5 %reduce-scatter.15.cloned.1.call-start = ((), (), s32[]{:S(2)}) async-start(), calls=%async_computation.11 | async-start | bytes 10027008 | tf_op jit(solution)/shard_map/reduce_scatter | solution.py:293
  1000.3 407.9 %reduce-scatter.17.cloned.1.call-start = ((), (), s32[]{:S(2)}) async-start(), calls=%async_computation.13 | async-start | bytes 10027008 | tf_op jit(solution)/shard_map/reduce_scatter | solution.py:294
  1008.1 475.0 %all-reduce.18.cloned.1.call-start = ((), (), s32[]{:S(2)}) async-start(), calls=%async_computation.22 | async-start | bytes 5013504 | tf_op jit(solution)/shard_map/psum | solution.py:300
  1408.2 84.6 %copy-start.76 = (f32[768]{0:T(1024)S(1)}, f32[768]{0:T(1024)}, u32[]{:S(2)}) copy-start(f32[768]{0:T(1024)} %get-tuple-element.1056) | copy-start | bytes 9220
  1408.2 84.6 %copy-start.94 = (f32[768]{0:T(1024)S(1)}, f32[768]{0:T(1024)}, u32[]{:S(2)}) copy-start(f32[768]{0:T(1024)} %get-tuple-element.1054) | copy-start | bytes 9220
  1408.2 84.7 %copy-start.95 = (f32[768]{0:T(1024)S(1)}, f32[768]{0:T(1024)}, u32[]{:S(2)}) copy-start(f32[768]{0:T(1024)} %get-tuple-element.1059) | copy-start | bytes 9220
  1408.2 216.3 %copy-start.25 = (bf16[768,768]{1,0:T(8,128)(2,1)S(1)}, bf16[768,768]{1,0:T(8,128)(2,1)}, u32[]{:S(2)}) copy-start(bf16[768,768]{1,0:T(8,128)(2,1)} %param.25) | copy-start | bytes 3538948
  1408.2 216.3 %copy-start.29 = (bf16[1,256,12,64]{1,3,2,0:T(8,128)(2,1)S(1)}, bf16[1,256,12,64]{1,3,2,0:T(8,128)(2,1)}, u32[]{:S(2)}) copy-start(bf16[1,256,12,64]{1,3,2,0:T(8,128)(2,1)} %copy-done.28) | copy-start | bytes 1179652
  1408.3 219.1 %all-gather.23.cloned.1.call-start = ((), (), s32[]{:S(2)}) async-start(), calls=%async_computation.6 | async-start | bytes 2506752 | tf_op jit(solution)/shard_map/all_gather | solution.py:316
  1484.9 142.4 %all-gather.25.cloned.1.call-start = ((), (), s32[]{:S(2)}) async-start(), calls=%async_computation.7 | async-start | bytes 2506752 | tf_op jit(solution)/shard_map/all_gather | solution.py:317
  1485.0 140.1 %copy-start.26 = (bf16[768,768]{1,0:T(8,128)(2,1)S(1)}, bf16[768,768]{1,0:T(8,128)(2,1)}, u32[]{:S(2)}) copy-start(bf16[768,768]{1,0:T(8,128)(2,1)} %param.26) | copy-start | bytes 3538948
  1486.9 140.5 %all-gather.27.cloned.1.call-start = ((), (), s32[]{:S(2)}) async-start(), calls=%async_computation.8 | async-start | bytes 2506752 | tf_op jit(solution)/shard_map/all_gather | solution.py:318
  1488.8 170.9 %all-gather.29.cloned.1.call-start = ((), (), s32[]{:S(2)}) async-start(), calls=%async_computation.10 | async-start | bytes 2506752 | tf_op jit(solution)/shard_map/all_gather | solution.py:319
  1489.4 252.1 %all-gather.31.cloned.1.call-start = ((), (), s32[]{:S(2)}) async-start(), calls=%async_computation.12 | async-start | bytes 10027008 | tf_op jit(solution)/shard_map/all_gather | solution.py:320
  1490.0 333.0 %all-gather.33.cloned.1.call-start = ((), (), s32[]{:S(2)}) async-start(), calls=%async_computation.14 | async-start | bytes 10027008 | tf_op jit(solution)/shard_map/all_gather | solution.py:321
  1627.4 199.0 %copy-start.40 = (f32[768,768]{1,0:T(8,128)S(1)}, f32[768,768]{1,0:T(8,128)}, u32[]{:S(2)}) copy-start(f32[768,768]{1,0:T(8,128)} %all-gather.25.cloned.1.call-done) | copy-start | bytes 7077892
  (148 other events, 604.5 us)
Sparse Core Ops, SparseCore 0:
  23.1 106.5 all-gather.36
  132.6 98.5 all-gather.34
  519.7 101.1 all-gather.40
  622.9 99.1 all-gather.38
  726.3 61.6 reduce-scatter.18
  982.5 62.3 reduce-scatter.20
  1049.2 62.1 reduce-scatter.22
  1115.7 62.1 reduce-scatter.12
  1182.6 110.2 reduce-scatter.14
  1297.4 110.8 reduce-scatter.16
  1411.4 71.6 all-reduce.17
  1485.8 42.5 all-gather.22
  1531.3 41.1 all-gather.24
  1575.2 41.1 all-gather.26
  1618.6 41.1 all-gather.28
  1661.9 79.6 all-gather.30
  1743.6 79.3 all-gather.32
where the time goes:
time: 1870 us; the launch traced here: 1850 us
  waiting for transfers between devices  741 us (40%)
  other arithmetic  311 us (17%)
  local copies, waits for them, and re-layouts  263 us (14%)
  blocking collectives  227 us (12%)
  loops' own time  205 us (11%)
  matrix products  84.1 us (4%)
    select_n x128, other arithmetic, hop(): return jax.tree.map(lambda a, b: jnp.where(reached, a, b), new, before)  219 us
    another operation x4, loops' own time, carried_in(): return lax.fori_loop(0, length, hop, start)  205 us
    dynamic_slice x192, local copies, waits for them, and re-layouts, hop(): new = combine(before, jax.tree.map(lambda part: part[at], everything))  191 us
    unnamed x3, blocking collectives  135 us
    reduce_scatter x1, waiting for transfers between devices, body(): lax.psum_scatter(local_grads[5], 'seq', scatter_dimension=0, tiled=True)  115 us
    reduce_scatter x1, waiting for transfers between devices, body(): lax.psum_scatter(local_grads[4], 'seq', scatter_dimension=0, tiled=True)  115 us
    unnamed x20, waiting for transfers between devices  103 us
    all_gather x4, blocking collectives, carried_in(): everything = jax.tree.map(lambda part: lax.all_gather(part, axis), value)  87.3 us
  transfers between devices with their start and end apart: 17, of which 11 were waited for; matrix products, arithmetic and copies ran while one was open for 25% of the time, Pallas kernels for 0%

commit v1 on v0

--- a/solution.py
+++ b/solution.py
@@ -7,6 +7,24 @@
 SEGS = 8
 EPSILON = 1e-06
 HIGHEST = lax.Precision.HIGHEST
+
+
+def gather_around(shard, axis, dim):
+    ways, here, step = (lax.axis_size(axis), lax.axis_index(axis), shard.shape[dim])
+    dims = [n * ways if d == dim else n for d, n in enumerate(shard.shape)]
+    full = lax.dynamic_update_slice_in_dim(
+        jnp.zeros(dims, shard.dtype), shard, here * step, axis=dim
+    )
+    going_up = going_down = shard
+    for far in range(1, ways // 2 + 1):
+        going_up = lax.ppermute(going_up, axis, [(d, (d + 1) % ways) for d in range(ways)])
+        full = lax.dynamic_update_slice_in_dim(full, going_up, (here - far) % ways * step, axis=dim)
+        if 2 * far < ways:
+            going_down = lax.ppermute(going_down, axis, [(d, (d - 1) % ways) for d in range(ways)])
+            full = lax.dynamic_update_slice_in_dim(
+                full, going_down, (here + far) % ways * step, axis=dim
+            )
+    return full
 
 
 def carried_in(value, axis, combine, identity, reverse):
@@ -318,7 +336,7 @@
         lax.all_gather(shares[2], "seq", axis=0, tiled=True),
         lax.all_gather(shares[3], "seq", axis=0, tiled=True),
         lax.all_gather(shares[4], "seq", axis=0, tiled=True),
-        lax.all_gather(shares[5], "seq", axis=0, tiled=True),
+        gather_around(shares[5], "seq", 0),
         lax.all_gather(shares[6], "seq", axis=0, tiled=True),
         lax.all_gather(shares[7], "seq", axis=0, tiled=True),
         lax.all_gather(shares[8], "seq", axis=0, tiled=True),

time: 1870 us -> 1820 us (0.973)
  waiting for transfers between devices: 741 us -> 635 us
  starting transfers between devices: 0.86 us -> 38 us
    all_gather x1 -> x0, waiting for transfers between devices: 81.5 us -> none  [body(): lax.all_gather(shares[5], 'seq', axis=0, tiled=True)]
    ppermute x0 -> x15, waiting for transfers between devices: none -> 66.4 us  [the longest x8 48.3 us: gather_around(): lax.ppermute(going_up, axis, [(d, (d + 1) % ways) for d in range(ways)])]
    all_gather x1, waiting for transfers between devices: 81.8 us -> 23.5 us  [body(): lax.all_gather(shares[4], 'seq', axis=0, tiled=True)]
    ppermute x0 -> x15, starting transfers between devices: none -> 37.2 us  [the longest x8 21.3 us: gather_around(): lax.ppermute(going_up, axis, [(d, (d + 1) % ways) for d in range(ways)])]
    all_gather x1, waiting for transfers between devices: 32.4 us -> 0.02 us  [body(): lax.all_gather(shares[3], 'seq', axis=0, tiled=True)]
    dynamic_update_slice x0 -> x16, local copies, waits for them, and re-layouts: none -> 21.3 us  [the longest x8 11.3 us: gather_around(): lax.dynamic_update_slice_in_dim(full, going_up, (here - far) % ways * ste...]
    unnamed x229 -> x236, local copies, waits for them, and re-layouts: 53.8 us -> 40.9 us
    unnamed x20 -> x19, waiting for transfers between devices: 103 us -> 101 us
  transfers between devices with their start and end apart: 17 -> 31, of which waited for: 11 -> 17; matrix products, arithmetic and copies ran while one was open for 25% -> 27% of each run, Pallas kernels for 0% -> 0%
where the time goes in v1:
time: 1820 us; the launch traced here: 1800 us
  waiting for transfers between devices  635 us (35%)
  other arithmetic  317 us (17%)
  local copies, waits for them, and re-layouts  276 us (15%)
  blocking collectives  226 us (12%)
  loops' own time  203 us (11%)
  matrix products  87.6 us (5%)
  starting transfers between devices  38 us (2%)
  between operations  18.2 us (1%)
    select_n x128, other arithmetic, hop(): return jax.tree.map(lambda a, b: jnp.where(reached, a, b), new, before)  221 us
    another operation x4, loops' own time, carried_in(): return lax.fori_loop(0, length, hop, start)  203 us
    dynamic_slice x192, local copies, waits for them, and re-layouts, hop(): new = combine(before, jax.tree.map(lambda part: part[at], everything))  190 us
    unnamed x3, blocking collectives  134 us
    reduce_scatter x1, waiting for transfers between devices, body(): lax.psum_scatter(local_grads[5], 'seq', scatter_dimension=0, tiled=True)  115 us
    reduce_scatter x1, waiting for transfers between devices, body(): lax.psum_scatter(local_grads[4], 'seq', scatter_dimension=0, tiled=True)  115 us
    unnamed x19, waiting for transfers between devices  101 us
    all_gather x4, blocking collectives, carried_in(): everything = jax.tree.map(lambda part: lax.all_gather(part, axis), value)  87.7 us
  transfers between devices with their start and end apart: 31, of which 17 were waited for; matrix products, arithmetic and copies ran while one was open for 27% of the time, Pallas kernels for 0%

profile of v1, /device:TPU:0, one launch (start us, length us, event | category | flops | bytes accessed | tf_op | source)
XLA Modules:
  0.0 1800.8 jit_solution(6635582913711101667)
XLA Ops:
  29.0 14.7 all-reduce.11
  51.6 21.3 %all-gather.9 = f32[16,12,256]{2,1,0:T(8,128)} all-gather(f32[1,12,256]{2,1,0:T(8,128)S(1)} %bitcast.471), channel_id=5, replica_groups=mesh['dp'=2,'seq'=16] {'seq'}, dimensions={0}, use_global_device_ids=true | all-gather | bytes 208896 | tf_op jit(solution)/shard_map/all_gather | solution.py:32
  72.9 22.4 %all-gather.8 = f32[16,12,256]{2,1,0:T(8,128)} all-gather(f32[1,12,256]{2,1,0:T(8,128)S(1)} %bitcast.470), channel_id=3, replica_groups=mesh['dp'=2,'seq'=16] {'seq'}, dimensions={0}, use_global_device_ids=true | all-gather | bytes 208896 | tf_op jit(solution)/shard_map/all_gather | solution.py:32
  98.3 31.4 %all-gather.34.cloned.1.call-done = f32[192,256,64]{1,2,0:T(8,128)} async-done(((f32[12,256,64]{1,2,0:T(8,128)}), f32[192,256,64]{1,2,0:T(8,128)}) %all-gather.34.cloned.1.call-update) | async-done | bytes 12582928 | tf_op jit(solution)/shard_map/all_gather | solution.py:32
  129.8 172.8 %while.77 = (s32[]{:T(128)}, f32[1,12,256,64]{3,2,1,0:T(8,128)}, f32[1,12,256]{2,1,0:T(8,128)}, s32[1]{0:T(128)}, s32[]{:T(128)}, /*index=5*/s32[16,1]{0,1:T(1,1...) while((s32[]{:T(128)}, f32[1,12,256,64]{3,2,1,0:T(8,128)}, ...), condition=%wide.region_8.9_spmd.clone, body=%wide.region_7.8_spmd.clone.sunk | while | flops 798738 | bytes 5640575 | solution.py:45
  305.4 174.7 %while.76 = (s32[]{:T(128)}, f32[1,12,256,64]{3,2,1,0:T(8,128)}, f32[1,12,256]{2,1,0:T(8,128)S(1)}, s32[1]{0:T(128)}, s32[]{:T(128)}, /*index=5*/s32[16,1]{0,1:T...) while((s32[]{:T(128)}, f32[1,12,256,64]{3,2,1,0:T(8,128)}, ...), condition=%wide.region_4.5_spmd.clone, body=%wide.region_3.4_spmd.clone.sunk | while | flops 798734 | bytes 5542153 | solution.py:45
  493.3 8.1 multiply_convert_fusion.2
  519.4 5.8 fusion.172
  534.3 23.0 %all-gather.11 = f32[16,12,256]{2,1,0:T(8,128)} all-gather(f32[1,12,256]{2,1,0:T(8,128)S(1)} %bitcast.469), channel_id=9, replica_groups=mesh['dp'=2,'seq'=16] {'seq'}, dimensions={0}, use_global_device_ids=true | all-gather | bytes 208896 | tf_op jit(solution)/shard_map/all_gather | solution.py:32
  557.3 21.0 %all-gather.10 = f32[16,12,256]{2,1,0:T(8,128)} all-gather(f32[1,12,256]{2,1,0:T(8,128)S(1)} %bitcast.468), channel_id=7, replica_groups=mesh['dp'=2,'seq'=16] {'seq'}, dimensions={0}, use_global_device_ids=true | all-gather | bytes 208896 | tf_op jit(solution)/shard_map/all_gather | solution.py:32
  578.4 42.0 %all-gather.38.cloned.1.call-done = f32[192,256,64]{1,2,0:T(8,128)} async-done(((f32[12,256,64]{1,2,0:T(8,128)}), f32[192,256,64]{1,2,0:T(8,128)}) %all-gather.38.cloned.1.call-update) | async-done | bytes 12582928 | tf_op jit(solution)/shard_map/all_gather | solution.py:32
  620.4 175.1 %while.79 = (s32[]{:T(128)}, f32[1,12,256,64]{3,2,1,0:T(8,128)}, f32[1,12,256]{2,1,0:T(8,128)}, s32[1]{0:T(128)}, s32[]{:T(128)}, /*index=5*/s32[16,1]{0,1:T(1,1...) while((s32[]{:T(128)}, f32[1,12,256,64]{3,2,1,0:T(8,128)}, ...), condition=%wide.region_29.30_spmd.clone, body=%wide.region_28.29_spmd.clone.sunk | while | flops 798738 | bytes 5640575 | solution.py:45
  795.5 173.0 %while.78 = (s32[]{:T(128)}, f32[1,12,256,64]{3,2,1,0:T(8,128)}, f32[1,12,256]{2,1,0:T(8,128)S(1)}, s32[1]{0:T(128)}, s32[]{:T(128)}, /*index=5*/s32[16,1]{0,1:T...) while((s32[]{:T(128)}, f32[1,12,256,64]{3,2,1,0:T(8,128)}, ...), condition=%wide.region_25.26_spmd.clone, body=%wide.region_24.25_spmd.clone.sunk | while | flops 798734 | bytes 5542153 | solution.py:45
  997.7 6.8 fusion.156
  1006.3 6.1 fusion.116
  1014.4 34.1 %reduce-scatter.21.cloned.1.call-done = f32[48,768]{1,0:T(8,128)} async-done(((f32[768,768]{1,0:T(8,128)}), f32[48,768]{1,0:T(8,128)}) %reduce-scatter.21.cloned.1.call-update) | async-done | bytes 147472
  1050.3 64.8 %reduce-scatter.23.cloned.1.call-done = f32[48,768]{1,0:T(8,128)} async-done(((f32[768,768]{1,0:T(8,128)}), f32[48,768]{1,0:T(8,128)}) %reduce-scatter.23.cloned.1.call-update) | async-done | bytes 147472
  1116.9 64.8 %reduce-scatter.13.cloned.1.call-done = f32[48,768]{1,0:T(8,128)} async-done(((f32[768,768]{1,0:T(8,128)}), f32[48,768]{1,0:T(8,128)}) %reduce-scatter.13.cloned.1.call-update) | async-done | bytes 147472 | tf_op jit(solution)/shard_map/reduce_scatter | solution.py:310
  1181.7 114.9 %reduce-scatter.15.cloned.1.call-done = f32[48,3072]{1,0:T(8,128)} async-done(((f32[768,3072]{1,0:T(8,128)}), f32[48,3072]{1,0:T(8,128)}) %reduce-scatter.15.cloned.1.call-update) | async-done | bytes 589840 | tf_op jit(solution)/shard_map/reduce_scatter | solution.py:311
  1296.6 115.4 %reduce-scatter.17.cloned.1.call-done = f32[192,768]{1,0:T(8,128)} async-done(((f32[3072,768]{1,0:T(8,128)}), f32[192,768]{1,0:T(8,128)}) %reduce-scatter.17.cloned.1.call-update) | async-done | bytes 589840 | tf_op jit(solution)/shard_map/reduce_scatter | solution.py:312
  1412.1 74.8 %all-reduce.18.cloned.1.call-done = (f32[48,768]{0,1:T(8,128)}, f32[48,768]{0,1:T(8,128)}, f32[48,768]{0,1:T(8,128)}, f32[48,768]{1,0:T(8,128)}, f32[48,3072]{1,0:T(8,128)}, /*index=5*/f32[192,768]{1,0:T(8,128)}) async-done(((f32[48,768]{0,1:T(8,128)}, f32[48,768]{0,1:T(8,128)}, f32[48,768]{0,1:T(8,128)}, f32[48,768]{1,0:T(8,128)}, f32[48,3072]{1,0:T(8,128)}, /*index=5*/f32[192,768]{1,0:T(8,128)}), ...) | async-done | bytes 1769488 | tf_op jit(solution)/shard_map/psum | solution.py:318
  1498.3 10.1 collective-permute-done
  1513.7 8.3 collective-permute-done.2
  1522.0 7.3 collective-permute-start.4
  1529.3 10.4 collective-permute-done.4
  1547.5 7.6 collective-permute-done.6
  1555.2 6.0 collective-permute-start.8
  1562.6 60.8 %all-reduce.13 = (f32[768]{0:T(1024)S(1)}, f32[768]{0:T(1024)S(1)}, f32[768]{0:T(1024)S(1)}, f32[768]{0:T(1024)S(1)}) all-reduce(f32[768]{0:T(1024)S(1)} %copy-done.98, f32[768]{0:T(1024)S(1)} %copy-done.99, f32[768]{0:T(1024)S(1)} %copy-done.80, f32[768]{0:T(1024)S(1)} %convert_reduce_fusion), channel_id=16, replica_groups=mesh['dp'=2,'seq'=16] {'seq'}, use_global_device_ids=true, to_apply=%region_45.46.clone | all-reduce | flops 3072 | bytes 24576
  1629.4 58.3 %all-reduce.12 = (f32[768]{0:T(1024)}, f32[768]{0:T(1024)}, f32[768]{0:T(1024)}, f32[768]{0:T(1024)}) all-reduce(f32[768]{0:T(1024)S(1)} %dynamic-update-slice.3, f32[768]{0:T(1024)S(1)} %dynamic-update-slice.4, f32[768]{0:T(1024)S(1)} %dynamic-update-slice.5, f32[768]{0:T(1024)S(1)} %dynamic-update-slice.6), channel_id=1, replica_groups=mesh['dp'=2,'seq'=16] {'seq'}, use_global_device_ids=true, to_apply=%add.3 | all-reduce | flops 3072 | bytes 24576
  1733.8 14.4 collective-permute-done.13
  1749.2 6.1 collective-permute-done.14
  1757.2 23.5 %all-gather.30.cloned.1.call-done = f32[768,3072]{1,0:T(8,128)} async-done(((f32[48,3072]{1,0:T(8,128)}), f32[768,3072]{1,0:T(8,128)}) %all-gather.30.cloned.1.call-update) | async-done | bytes 9437200 | tf_op jit(solution)/shard_map/all_gather | solution.py:338
  (909 shorter events, 695.1 us)
Async XLA Ops:
  7.2 484.1 %copy-start = (bf16[768,768]{1,0:T(8,128)(2,1)S(1)}, bf16[768,768]{1,0:T(8,128)(2,1)}, u32[]{:S(2)}) copy-start(bf16[768,768]{1,0:T(8,128)(2,1)} %param.28) | copy-start | bytes 3538948
  7.2 122.6 %all-gather.34.cloned.1.call-start = ((), (), s32[]{:S(2)}) async-start(), calls=%async_computation.15 | async-start | bytes 13369344 | tf_op jit(solution)/shard_map/all_gather | solution.py:32
  23.0 282.3 %all-gather.32.cloned.1.call-start = ((), (), s32[]{:S(2)}) async-start(), calls=%async_computation.14 | async-start | bytes 13369344 | tf_op jit(solution)/shard_map/all_gather | solution.py:32
  23.8 596.6 %all-gather.38.cloned.1.call-start = ((), (), s32[]{:S(2)}) async-start(), calls=%async_computation.17 | async-start | bytes 13369344 | tf_op jit(solution)/shard_map/all_gather | solution.py:32
  518.6 276.9 %all-gather.36.cloned.1.call-start = ((), (), s32[]{:S(2)}) async-start(), calls=%async_computation.16 | async-start | bytes 13369344 | tf_op jit(solution)/shard_map/all_gather | solution.py:32
  519.2 493.3 %reduce-scatter.19.cloned.1.call-start = ((), (), s32[]{:S(2)}) async-start(), calls=%async_computation.18 | async-start | bytes 2506752
  578.3 470.1 %reduce-scatter.21.cloned.1.call-start = ((), (), s32[]{:S(2)}) async-start(), calls=%async_computation.19 | async-start | bytes 2506752
  986.6 128.4 %reduce-scatter.23.cloned.1.call-start = ((), (), s32[]{:S(2)}) async-start(), calls=%async_computation.20 | async-start | bytes 2506752
  995.5 186.2 %reduce-scatter.13.cloned.1.call-start = ((), (), s32[]{:S(2)}) async-start(), calls=%async_computation.9 | async-start | bytes 2506752 | tf_op jit(solution)/shard_map/reduce_scatter | solution.py:310
  997.6 299.0 %reduce-scatter.15.cloned.1.call-start = ((), (), s32[]{:S(2)}) async-start(), calls=%async_computation.11 | async-start | bytes 10027008 | tf_op jit(solution)/shard_map/reduce_scatter | solution.py:311
  1004.6 407.4 %reduce-scatter.17.cloned.1.call-start = ((), (), s32[]{:S(2)}) async-start(), calls=%async_computation.13 | async-start | bytes 10027008 | tf_op jit(solution)/shard_map/reduce_scatter | solution.py:312
  1012.4 474.5 %all-reduce.18.cloned.1.call-start = ((), (), s32[]{:S(2)}) async-start(), calls=%async_computation.21 | async-start | bytes 5013504 | tf_op jit(solution)/shard_map/psum | solution.py:318
  1412.1 337.1 %all-gather.22.cloned.1.call-start = ((), (), s32[]{:S(2)}) async-start(), calls=%async_computation.6 | async-start | bytes 2506752 | tf_op jit(solution)/shard_map/all_gather | solution.py:334
  1488.8 260.4 %all-gather.24.cloned.1.call-start = ((), (), s32[]{:S(2)}) async-start(), calls=%async_computation.7 | async-start | bytes 2506752 | tf_op jit(solution)/shard_map/all_gather | solution.py:335
  1490.7 258.4 %all-gather.26.cloned.1.call-start = ((), (), s32[]{:S(2)}) async-start(), calls=%async_computation.8 | async-start | bytes 2506752 | tf_op jit(solution)/shard_map/all_gather | solution.py:336
  1492.6 256.5 %all-gather.28.cloned.1.call-start = ((), (), s32[]{:S(2)}) async-start(), calls=%async_computation.10 | async-start | bytes 2506752 | tf_op jit(solution)/shard_map/all_gather | solution.py:337
  1493.2 287.5 %all-gather.30.cloned.1.call-start = ((), (), s32[]{:S(2)}) async-start(), calls=%async_computation.12 | async-start | bytes 10027008 | tf_op jit(solution)/shard_map/all_gather | solution.py:338
  1493.8 14.6 collective-permute-start
  1493.8 17.4 collective-permute-start.1
  1509.2 12.8 collective-permute-start.2
  1511.3 18.0 collective-permute-start.3
  1522.0 17.7 collective-permute-start.4
  1529.3 18.2 %collective-permute-start.5 = (f32[192,768]{1,0:T(8,128)}, f32[192,768]{1,0:T(8,128)}, u32[]{:S(2)}, u32[]{:S(2)}) collective-permute-start(f32[192,768]{1,0:T(8,128)} %collective-permute-done.3), channel_id=1, source_target_pairs={{0,15},{1,0},{2,1},{3,2},{4,3},{5,4},{6,5},{7,6},{8,7},{9,8},{10,9... | collective-permute-start | bytes 1769480 | tf_op jit(solution)/shard_map/ppermute | solution.py:23
  1539.7 15.5 collective-permute-start.6
  1547.5 141.9 %collective-permute-start.7 = (f32[192,768]{1,0:T(8,128)}, f32[192,768]{1,0:T(8,128)}, u32[]{:S(2)}, u32[]{:S(2)}) collective-permute-start(f32[192,768]{1,0:T(8,128)} %collective-permute-done.5), channel_id=1, source_target_pairs={{0,15},{1,0},{2,1},{3,2},{4,3},{5,4},{6,5},{7,6},{8,7},{9,8},{10,9... | collective-permute-start | bytes 1769480 | tf_op jit(solution)/shard_map/ppermute | solution.py:23
  1555.2 137.0 %collective-permute-start.8 = (f32[192,768]{1,0:T(8,128)}, f32[192,768]{1,0:T(8,128)}, u32[]{:S(2)}, u32[]{:S(2)}) collective-permute-start(f32[192,768]{1,0:T(8,128)} %collective-permute-done.6), channel_id=1, source_target_pairs={{0,1},{1,2},{2,3},{3,4},{4,5},{5,6},{6,7},{7,8},{8,9},{9,10},{10,1... | collective-permute-start | bytes 1769480 | tf_op jit(solution)/shard_map/ppermute | solution.py:20
  1689.4 14.7 collective-permute-start.9
  1692.2 24.0 %collective-permute-start.10 = (f32[192,768]{1,0:T(8,128)}, f32[192,768]{1,0:T(8,128)S(1)}, u32[]{:S(2)}, u32[]{:S(2)}) collective-permute-start(f32[192,768]{1,0:T(8,128)} %collective-permute-done.8), channel_id=1, source_target_pairs={{0,1},{1,2},{2,3},{3,4},{4,5},{5,6},{6,7},{7,8},{8,9},{9,10},{10,1... | collective-permute-start | bytes 1769480 | tf_op jit(solution)/shard_map/ppermute | solution.py:20
  1704.1 19.7 %collective-permute-start.11 = (f32[192,768]{1,0:T(8,128)S(1)}, f32[192,768]{1,0:T(8,128)S(1)}, u32[]{:S(2)}, u32[]{:S(2)}) collective-permute-start(f32[192,768]{1,0:T(8,128)S(1)} %collective-permute-done.9), channel_id=1, source_target_pairs={{0,15},{1,0},{2,1},{3,2},{4,3},{5,4},{6,5},{7,6},{8,7},{9,8},{10,9... | collective-permute-start | bytes 1769480 | tf_op jit(solution)/shard_map/ppermute | solution.py:23
  1716.2 14.2 collective-permute-start.12
  1723.9 24.4 %collective-permute-start.13 = (f32[192,768]{1,0:T(8,128)S(1)}, f32[192,768]{1,0:T(8,128)S(1)}, u32[]{:S(2)}, u32[]{:S(2)}) collective-permute-start(f32[192,768]{1,0:T(8,128)S(1)} %collective-permute-done.11), channel_id=1, source_target_pairs={{0,15},{1,0},{2,1},{3,2},{4,3},{5,4},{6,5},{7,6},{8,7},{9,8},{10,9... | collective-permute-start | bytes 1769480 | tf_op jit(solution)/shard_map/ppermute | solution.py:23
  1730.4 24.9 %collective-permute-start.14 = (f32[192,768]{1,0:T(8,128)S(1)}, f32[192,768]{1,0:T(8,128)}, u32[]{:S(2)}, u32[]{:S(2)}) collective-permute-start(f32[192,768]{1,0:T(8,128)S(1)} %collective-permute-done.12), channel_id=1, source_target_pairs={{0,1},{1,2},{2,3},{3,4},{4,5},{5,6},{6,7},{7,8},{8,9},{9,10},{10,1... | collective-permute-start | bytes 1769480 | tf_op jit(solution)/shard_map/ppermute | solution.py:20
  (166 other events, 2214.3 us)
Sparse Core Ops, SparseCore 0:
  23.1 106.6 all-gather.33
  132.6 98.6 all-gather.31
  518.7 101.6 all-gather.37
  622.5 99.2 all-gather.35
  726.0 61.4 reduce-scatter.18
  986.8 61.6 reduce-scatter.20
  1052.8 62.2 reduce-scatter.22
  1119.4 62.2 reduce-scatter.12
  1186.4 110.2 reduce-scatter.14
  1301.1 110.8 reduce-scatter.16
  1415.3 71.6 all-reduce.17
  1489.6 59.3 all-gather.21
  1551.3 45.4 all-gather.23
  1599.0 41.2 all-gather.25
  1642.4 41.7 all-gather.27
  1686.3 94.3 all-gather.29
